TPU v7x, 32 devices: a whole 2x2x4 slice. The times are simulated.
32 devices in a mesh: grp: 2 (over y), leaf: 16 (over z, x, core).
Axes of the slice: x: 2, y: 2, z: 4, core: 2. Of those that a mesh axis runs over, the one named last changes fastest.
Arguments:
- vectors: float32 [16, 32768], P(None, ('grp', 'leaf')), may hold values from -6 to 6
- points: float32 [3, 32768], P(None, ('grp', 'leaf')), may hold values from -1 to 2
- near_lists: int32 [64, 6], P(('grp', 'leaf')), may hold values from -1 to 5, as said below
- inter_lists: int32 [64, 16], P(('grp', 'leaf')), may hold values from 0 to 31, as said below
- skeleton: int32 [64, 64], P(('grp', 'leaf')), may hold values from 0 to 511, as said below
- interp: float32 [64, 64, 512], P(('grp', 'leaf')), may hold values from -0.25 to 0.25
- transfer: float32 [64, 64, 128], P(('grp', 'leaf')), may hold values from -0.125 to 0.125
- coarse_points: float32 [2, 3, 128], replicated, may hold values from 0 to 1
Outputs:
- filtered: float32 [16, 32768], P(None, ('grp', 'leaf'))
Inputs may be any that keep to these rules, and one draw needn't show every extreme that they name: `near_lists`: place w of leaf l's window is leaf (l // 2 - 1) * 2 + w. Slot 0 holds the leaf itself (2 + l % 2); the next slots hold distinct places of other leaves of the same subtree; then -1 to the end of the row. `inter_lists`: distinct leaves of the leaf's own subtree, numbered from the subtree's first leaf, none in the leaf's window. `skeleton`: distinct places within the leaf.
All inputs are finite; a program needn't handle non-finite values.
Results may differ from a plain program's by a relative error of at most 0.00013.
Values sent between devices are 32-bit elements; how exact they have to be, the bound alone decides.
No kernel may reach another device: no remote copies, remote signals or barrier semaphores. Data moves between devices by JAX's collectives and lax.ppermute only.
A program may use at most 64 MiB of HBM per device.

v0:
```python
import jax
import jax.numpy as jnp
from jax import lax
from jax.sharding import PartitionSpec as P

kappa_scale = 3.4641016151377544
centre = 0.05
half_width = 0.05
highest = lax.Precision.HIGHEST


def with_halo(x, sides, width):
    for axis, dim in sides:
        devices, length = (lax.axis_size(axis), x.shape[dim])
        up = [(i, (i + 1) % devices) for i in range(devices - 1)]
        down = [(j, i) for i, j in up]
        last = lax.slice_in_dim(x, length - width, length, axis=dim)
        initial = lax.slice_in_dim(x, 0, width, axis=dim)
        before = lax.ppermute(last, axis, up)
        after = lax.ppermute(initial, axis, down)
        x = jnp.concatenate([before, x, after], axis=dim)
    return x


def matern(source, target):
    delta_x = source[..., 0, :, None] - target[..., 0, None, :]
    delta_y = source[..., 1, :, None] - target[..., 1, None, :]
    delta_z = source[..., 2, :, None] - target[..., 2, None, :]
    scaled = kappa_scale * jnp.sqrt(delta_x * delta_x + delta_y * delta_y + delta_z * delta_z)
    return (1.0 + scaled) * jnp.exp(-scaled)


def on_device(vectors, points, near_lists, inter_lists, skeleton, interp, transfer, coarse_points):
    per_dev = near_lists.shape[0]
    slot_count = near_lists.shape[1]
    leaf_size = interp.shape[2]
    vec_count = vectors.shape[0]
    leaf_index = lax.axis_index("leaf")
    group_index = lax.axis_index("grp")
    group_count = lax.axis_size("grp")
    leaf_points = points.reshape(3, per_dev, leaf_size).transpose(1, 0, 2)
    skel_points = jnp.take_along_axis(leaf_points, skeleton[:, None, :], axis=2)
    subtree_skel = lax.all_gather(skel_points, "leaf", axis=0, tiled=True)
    own_coarse = lax.dynamic_index_in_dim(coarse_points, group_index, 0, keepdims=False)
    apart = (jnp.arange(group_count) != group_index).astype(jnp.float32)
    coupling = matern(coarse_points, own_coarse[None]) * apart[:, None, None]
    live_slots = jnp.max(jnp.sum((near_lists >= 0).astype(jnp.int32), axis=1))
    first_leaf = leaf_index * per_dev
    subtree_lists = lax.all_gather(inter_lists, "leaf", axis=0, tiled=True)
    own_ids = first_leaf + jnp.arange(per_dev, dtype=jnp.int32)
    hits = jnp.sum(
        (subtree_lists[:, :, None] == own_ids[None, None, :]).astype(jnp.float32), axis=1
    )
    push_kernel = matern(skel_points[None], subtree_skel[:, None]) * hits[:, :, None, None]

    def operate(field):
        stacked = jnp.concatenate([points, field], axis=0)
        window = with_halo(stacked, (("leaf", 1),), per_dev * leaf_size)
        window_points = window[:3].reshape(3, 3 * per_dev, leaf_size)
        window_vecs = window[3:].reshape(vec_count, 3 * per_dev, leaf_size)

        def near_slot(slot, running):
            chosen = lax.dynamic_index_in_dim(near_lists, slot, 1, keepdims=False)
            present = (chosen >= 0).astype(jnp.float32)
            safe_place = jnp.where(chosen >= 0, chosen, 0)
            source_points = jnp.take(window_points, safe_place, axis=1).transpose(1, 0, 2)
            source_vecs = jnp.take(window_vecs, safe_place, axis=1)
            kernel = matern(source_points, leaf_points)
            product = jnp.einsum("vlp,lpq->lvq", source_vecs, kernel, precision=highest)
            return running + present[:, None, None] * product

        near_part = lax.fori_loop(
            0, live_slots, near_slot, jnp.zeros((per_dev, vec_count, leaf_size), jnp.float32)
        )
        leaf_vecs = field.reshape(vec_count, per_dev, leaf_size)
        coeffs = jnp.einsum("vlp,lrp->lvr", leaf_vecs, interp, precision=highest)
        leaf_far = lax.psum_scatter(
            jnp.einsum("jvr,tjrq->tvq", coeffs, push_kernel, precision=highest),
            "leaf",
            scatter_dimension=0,
            tiled=True,
        )
        upward = jnp.einsum("lvr,lrc->vc", coeffs, transfer, precision=highest)
        subtree_total = lax.psum(upward, "leaf")
        group_coeffs = lax.all_gather(subtree_total[None], "grp", axis=0, tiled=True)
        coarse_field = jnp.einsum("avr,arq->vq", group_coeffs, coupling, precision=highest)
        downward = leaf_far + jnp.einsum("vc,lrc->lvr", coarse_field, transfer, precision=highest)
        far_part = jnp.einsum("lvr,lrp->lvp", downward, interp, precision=highest)
        combined = (near_part + far_part) / (leaf_size * slot_count)
        return combined.transpose(1, 0, 2).reshape(vec_count, per_dev * leaf_size)

    term_one = (operate(vectors) - centre * vectors) / half_width
    term_two = 2.0 * (operate(term_one) - centre * term_one) / half_width - vectors
    term_three = 2.0 * (operate(term_two) - centre * term_two) / half_width - term_one
    squares = lax.psum(jnp.sum(term_three * term_three, axis=1), ("grp", "leaf"))
    total_points = vectors.shape[1] * group_count * lax.axis_size("leaf")
    return term_three / jnp.sqrt(squares / total_points + 1e-06)[:, None]


def solution(mesh):
    placed = (
        P(None, ("grp", "leaf")),
        P(None, ("grp", "leaf")),
        P(("grp", "leaf"), None),
        P(("grp", "leaf"), None),
        P(("grp", "leaf"), None),
        P(("grp", "leaf"), None, None),
        P(("grp", "leaf"), None, None),
        P(),
    )
    return jax.shard_map(
        on_device, mesh=mesh, in_specs=placed, out_specs=P(None, ("grp", "leaf")), check_vma=False
    )
```

profile of v0, /device:TPU:10, one launch (start us, length us, event | category | flops | bytes accessed | tf_op | source)
XLA Modules:
  0.0 312.5 jit_solution(3287674258489741425)
XLA Ops:
  14.4 15.5 %all-gather = s32[16,2,16]{2,1,0:T(2,128)S(1)} all-gather(s32[1,2,16]{2,1,0:T(2,128)S(1)} %bitcast.260), channel_id=1, replica_groups=mesh['grp'=2,'leaf'=16] {'leaf'}, dimensions={0}, use_global_device_ids=true | all-gather | bytes 2176 | tf_op jit(solution)/shard_map/all_gather | solution.py:49
  30.1 21.1 %all_gather.15 = f32[32,3,64]{2,1,0:T(4,128)S(1)} all-gather(f32[2,3,64]{2,1,0:T(4,128)S(1)} %bitcast_select_fusion.1), channel_id=1, replica_groups=mesh['grp'=2,'leaf'=16] {'leaf'}, dimensions={0}, use_global_device_ids=true | all-gather | bytes 26112 | tf_op jit(solution)/shard_map/all_gather | solution.py:43
  51.6 3.5 %convolution_bitcast_fusion.2 = f32[32,16,64]{2,1,0:T(8,128)} fusion(f32[32,2]{1,0:T(8,128)S(1)} %copy.67, f32[32,64]{1,0:T(8,128)S(1)} %bitcast.254, f32[2,64]{1,0:T(2,128)S(1)} %bitcast.264, f32[32,64]{1,0:T(8,128)S(1)} %bitcast.257, f32[2,64]{1,0:T(2,128)S(1)} %bitcast.267, f32[32,64]{1,0:T(8,128)S(1)} %bitcast.251, f32[2,64]{1,0:T(2,128)S(1)} %bitcast.261, ...), kind=kOutput, calls=%fused_computation.145 | convolution fusion | flops 53739520 | bytes 165632 | tf_op jit(solution)/shard_map/jvr,tjrq->tvq/dot_general | solution.py:78
  56.1 24.3 %psum.28 = f32[1,16,128]{2,1,0:T(8,128)S(1)} all-reduce(f32[1,16,128]{2,1,0:T(8,128)S(1)} %convolution_bitcast_fusion.8), channel_id=1, replica_groups=mesh['grp'=2,'leaf'=16] {'leaf'}, use_global_device_ids=true, to_apply=%region_6.9 | all-reduce | flops 2048 | bytes 16384 | tf_op jit(solution)/shard_map/psum | solution.py:84
  80.4 4.4 %all_gather.17 = f32[2,16,128]{2,1,0:T(8,128)S(1)} all-gather(f32[1,16,128]{2,1,0:T(8,128)S(1)} %psum.28), channel_id=1, replica_groups=mesh['grp'=2,'leaf'=16] {'grp'}, dimensions={0}, use_global_device_ids=true | all-gather | bytes 24576 | tf_op jit(solution)/shard_map/all_gather | solution.py:85
  86.1 28.6 %while.30 = (s32[]{:T(128)}, f32[2,16,512]{2,1,0:T(8,128)S(1)}, s32[]{:T(128)}, s32[2,6]{0,1:T(8,128)S(1)}, f32[16,6,512]{2,0,1:T(8,128)S(1)}, /*index=5*/f32[3,...) while((s32[]{:T(128)}, f32[2,16,512]{2,1,0:T(8,128)S(1)}, s32[]{:T(128)}, ...), condition=%wide.region_3.0_spmd, body=%wide.region_2.0_spmd.sunk | while | flops 107008024 | bytes 479441 | solution.py:72
  87.9 2.8 fusion.199
  92.6 2.8 fusion.199
  97.3 2.8 fusion.199
  102.0 2.8 fusion.199
  106.6 2.8 fusion.199
  111.3 2.8 fusion.199
  120.7 3.5 %convolution_bitcast_fusion.1 = f32[32,16,64]{2,1,0:T(8,128)} fusion(f32[32,2]{1,0:T(8,128)S(1)} %copy.67, f32[32,64]{1,0:T(8,128)S(1)} %bitcast.255, f32[2,64]{1,0:T(2,128)S(1)} %bitcast.265, f32[32,64]{1,0:T(8,128)S(1)} %bitcast.258, f32[2,64]{1,0:T(2,128)S(1)} %bitcast.268, f32[32,64]{1,0:T(8,128)S(1)} %bitcast.252, f32[2,64]{1,0:T(2,128)S(1)} %bitcast.262, ...), kind=kOutput, calls=%fused_computation.144 | convolution fusion | flops 53739520 | bytes 165632 | tf_op jit(solution)/shard_map/jvr,tjrq->tvq/dot_general | solution.py:78
  124.4 26.7 %psum.29 = f32[1,16,128]{2,1,0:T(8,128)S(1)} all-reduce(f32[1,16,128]{2,1,0:T(8,128)S(1)} %convolution_bitcast_fusion.7), channel_id=1, replica_groups=mesh['grp'=2,'leaf'=16] {'leaf'}, use_global_device_ids=true, to_apply=%region_10.13 | all-reduce | flops 2048 | bytes 16384 | tf_op jit(solution)/shard_map/psum | solution.py:84
  151.2 4.4 %all_gather.18 = f32[2,16,128]{2,1,0:T(8,128)S(1)} all-gather(f32[1,16,128]{2,1,0:T(8,128)S(1)} %psum.29), channel_id=1, replica_groups=mesh['grp'=2,'leaf'=16] {'grp'}, dimensions={0}, use_global_device_ids=true | all-gather | bytes 24576 | tf_op jit(solution)/shard_map/all_gather | solution.py:85
  156.0 28.8 %while.31 = (s32[]{:T(128)}, f32[2,16,512]{2,1,0:T(8,128)S(1)}, s32[]{:T(128)}, s32[2,6]{0,1:T(8,128)S(1)}, f32[16,6,512]{2,0,1:T(8,128)S(1)}, /*index=5*/f32[3,...) while((s32[]{:T(128)}, f32[2,16,512]{2,1,0:T(8,128)S(1)}, s32[]{:T(128)}, ...), condition=%wide.region_8.11_spmd, body=%wide.region_7.10_spmd.sunk | while | flops 107008024 | bytes 479441 | solution.py:72
  158.1 2.8 fusion.203
  162.7 2.8 fusion.203
  167.4 2.8 fusion.203
  172.1 2.8 fusion.203
  176.8 2.8 fusion.203
  181.4 2.8 fusion.203
  191.3 3.5 %convolution_bitcast_fusion = f32[32,16,64]{2,1,0:T(8,128)} fusion(f32[32,2]{1,0:T(8,128)S(1)} %copy.67, f32[32,64]{1,0:T(8,128)S(1)} %bitcast.256, f32[2,64]{1,0:T(2,128)S(1)} %bitcast.266, f32[32,64]{1,0:T(8,128)S(1)} %bitcast.259, f32[2,64]{1,0:T(2,128)S(1)} %bitcast.269, f32[32,64]{1,0:T(8,128)S(1)} %bitcast.253, f32[2,64]{1,0:T(2,128)S(1)} %bitcast.263, ...), kind=kOutput, calls=%fused_computation.143 | convolution fusion | flops 53739520 | bytes 165632 | tf_op jit(solution)/shard_map/jvr,tjrq->tvq/dot_general | solution.py:78
  195.0 28.1 %psum.30 = f32[1,16,128]{2,1,0:T(8,128)S(1)} all-reduce(f32[1,16,128]{2,1,0:T(8,128)S(1)} %convolution_bitcast_fusion.6), channel_id=1, replica_groups=mesh['grp'=2,'leaf'=16] {'leaf'}, use_global_device_ids=true, to_apply=%region_14.17 | all-reduce | flops 2048 | bytes 16384 | tf_op jit(solution)/shard_map/psum | solution.py:84
  223.1 4.4 %all_gather.19 = f32[2,16,128]{2,1,0:T(8,128)S(1)} all-gather(f32[1,16,128]{2,1,0:T(8,128)S(1)} %psum.30), channel_id=1, replica_groups=mesh['grp'=2,'leaf'=16] {'grp'}, dimensions={0}, use_global_device_ids=true | all-gather | bytes 24576 | tf_op jit(solution)/shard_map/all_gather | solution.py:85
  227.9 28.6 %while.32 = (s32[]{:T(128)}, f32[2,16,512]{2,1,0:T(8,128)S(1)}, s32[]{:T(128)}, s32[2,6]{0,1:T(8,128)S(1)}, f32[16,6,512]{2,0,1:T(8,128)S(1)}, /*index=5*/f32[3,...) while((s32[]{:T(128)}, f32[2,16,512]{2,1,0:T(8,128)S(1)}, s32[]{:T(128)}, ...), condition=%wide.region_12.15_spmd, body=%wide.region_11.14_spmd.sunk | while | flops 107008024 | bytes 479441 | solution.py:72
  229.8 2.8 fusion.207
  234.5 2.8 fusion.207
  239.2 2.8 fusion.207
  243.8 2.8 fusion.207
  248.5 2.8 fusion.207
  258.7 46.5 %psum.31 = f32[16]{0:T(128)S(1)} all-reduce(f32[16]{0:T(128)S(1)} %multiply_reduce_fusion), channel_id=1, replica_groups=mesh['grp'=2,'leaf'=16] {'grp','leaf'}, use_global_device_ids=true, to_apply=%region_16.19 | all-reduce | flops 16 | bytes 128 | tf_op jit(solution)/shard_map/psum | solution.py:95
  (244 shorter events, 52.2 us)
Async XLA Ops:
  6.5 44.8 %copy-start = (f32[2,64,512]{2,1,0:T(8,128)S(1)}, f32[2,64,512]{2,1,0:T(8,128)}, u32[]{:S(2)}) copy-start(f32[2,64,512]{2,1,0:T(8,128)} %param.23) | copy-start | bytes 786436
  6.5 6.4 %copy-start.7 = (s32[2,64]{1,0:T(2,128)S(1)}, s32[2,64]{1,0:T(2,128)}, u32[]{:S(2)}) copy-start(s32[2,64]{1,0:T(2,128)} %param.22) | copy-start | bytes 1540
  6.5 7.8 %copy-start.5 = (s32[2,16]{1,0:T(2,128)S(1)}, s32[2,16]{1,0:T(2,128)}, u32[]{:S(2)}) copy-start(s32[2,16]{1,0:T(2,128)} %param.21) | copy-start | bytes 388
  6.5 108.2 %reduce-scatter.4.cloned.1.call-start = ((), (), s32[]{:S(2)}) async-start(), calls=%async_computation.3 | async-start | bytes 278528 | tf_op jit(solution)/shard_map/reduce_scatter | solution.py:77
  7.5 43.8 %copy-start.2 = (f32[16,1024]{1,0:T(8,128)S(1)}, f32[16,1024]{1,0:T(8,128)}, u32[]{:S(2)}) copy-start(f32[16,1024]{1,0:T(8,128)} %param.18) | copy-start | bytes 196612
  7.5 78.5 %collective-permute-start.1 = (f32[19,1024]{1,0:T(8,128)S(1)}, f32[19,1024]{1,0:T(8,128)S(1)}, u32[]{:S(2)}, u32[]{:S(2)}) collective-permute-start(f32[19,1024]{1,0:T(8,128)S(1)} %pad_maximum_fusion.3), channel_id=1, source_target_pairs={{1,0},{2,1},{3,2},{4,3},{5,4},{6,5},{7,6},{8,7},{9,8},{10,9},{11,1... | collective-permute-start | bytes 233480 | tf_op jit(solution)/shard_map/ppermute | solution.py:20
  9.5 76.4 %collective-permute-start = (f32[19,1024]{1,0:T(8,128)S(1)}, f32[19,1024]{1,0:T(8,128)S(1)}, u32[]{:S(2)}, u32[]{:S(2)}) collective-permute-start(f32[19,1024]{1,0:T(8,128)S(1)} %pad_maximum_fusion.3), channel_id=1, source_target_pairs={{0,1},{1,2},{2,3},{3,4},{4,5},{5,6},{6,7},{7,8},{8,9},{9,10},{10,1... | collective-permute-start | bytes 233480 | tf_op jit(solution)/shard_map/ppermute | solution.py:19
  55.1 0.7 copy-start.6
  55.1 0.9 copy-start.1
  55.1 29.7 %copy-start.4 = (f32[2,3,128]{2,0,1:T(2,128)S(1)}, f32[2,3,128]{2,0,1:T(2,128)}, u32[]{:S(2)}) copy-start(f32[2,3,128]{2,0,1:T(2,128)} %param.25) | copy-start | bytes 9220
  55.1 30.8 %copy-start.3 = (f32[3,1024]{1,0:T(4,128)S(1)}, f32[3,1024]{1,0:T(4,128)}, u32[]{:S(2)}) copy-start(f32[3,1024]{1,0:T(4,128)} %param.19) | copy-start | bytes 36868
  55.1 130.2 %reduce-scatter.6.cloned.1.call-start = ((), (), s32[]{:S(2)}) async-start(), calls=%async_computation.4 | async-start | bytes 278528 | tf_op jit(solution)/shard_map/reduce_scatter | solution.py:77
  116.0 39.9 %collective-permute-start.3 = (f32[19,1024]{1,0:T(8,128)S(1)}, f32[19,1024]{1,0:T(8,128)S(1)}, u32[]{:S(2)}, u32[]{:S(2)}) collective-permute-start(f32[19,1024]{1,0:T(8,128)S(1)} %pad_maximum_fusion.4), channel_id=1, source_target_pairs={{1,0},{2,1},{3,2},{4,3},{5,4},{6,5},{7,6},{8,7},{9,8},{10,9},{11,1... | collective-permute-start | bytes 233480 | tf_op jit(solution)/shard_map/ppermute | solution.py:20
  117.9 38.0 %collective-permute-start.2 = (f32[19,1024]{1,0:T(8,128)S(1)}, f32[19,1024]{1,0:T(8,128)S(1)}, u32[]{:S(2)}, u32[]{:S(2)}) collective-permute-start(f32[19,1024]{1,0:T(8,128)S(1)} %pad_maximum_fusion.4), channel_id=1, source_target_pairs={{0,1},{1,2},{2,3},{3,4},{4,5},{5,6},{6,7},{7,8},{8,9},{9,10},{10,1... | collective-permute-start | bytes 233480 | tf_op jit(solution)/shard_map/ppermute | solution.py:19
  124.4 132.9 %reduce-scatter.8.cloned.1.call-start = ((), (), s32[]{:S(2)}) async-start(), calls=%async_computation.5 | async-start | bytes 278528 | tf_op jit(solution)/shard_map/reduce_scatter | solution.py:77
  186.6 41.2 %collective-permute-start.5 = (f32[19,1024]{1,0:T(8,128)S(1)}, f32[19,1024]{1,0:T(8,128)S(1)}, u32[]{:S(2)}, u32[]{:S(2)}) collective-permute-start(f32[19,1024]{1,0:T(8,128)S(1)} %pad_maximum_fusion.5), channel_id=1, source_target_pairs={{1,0},{2,1},{3,2},{4,3},{5,4},{6,5},{7,6},{8,7},{9,8},{10,9},{11,1... | collective-permute-start | bytes 233480 | tf_op jit(solution)/shard_map/ppermute | solution.py:20
  188.5 39.3 %collective-permute-start.4 = (f32[19,1024]{1,0:T(8,128)S(1)}, f32[19,1024]{1,0:T(8,128)S(1)}, u32[]{:S(2)}, u32[]{:S(2)}) collective-permute-start(f32[19,1024]{1,0:T(8,128)S(1)} %pad_maximum_fusion.5), channel_id=1, source_target_pairs={{0,1},{1,2},{2,3},{3,4},{4,5},{5,6},{6,7},{7,8},{8,9},{9,10},{10,1... | collective-permute-start | bytes 233480 | tf_op jit(solution)/shard_map/ppermute | solution.py:19
Sparse Core Ops, SparseCore 0:
  55.2 56.6 reduce-scatter.3
  124.5 60.7 reduce-scatter.5
  195.1 62.1 reduce-scatter.7
where the time goes:
time: 313 us; the launch traced here: 312 us
  blocking collectives  175 us (56%)
  matrix products  66.6 us (21%)
  local copies, waits for them, and re-layouts  24.2 us (8%)
  loops' own time  13.7 us (4%)
  between operations  13.7 us (4%)
  starting transfers between devices  13.2 us (4%)
  other arithmetic  4.5 us (1%)
    psum x3, blocking collectives, operate(): subtree_total = lax.psum(upward, 'leaf')  79.1 us
    dot_general x18, matrix products, near_slot(): product = jnp.einsum('vlp,lpq->lvq', source_vecs, kernel, precision=highest)  50 us
    psum x1, blocking collectives, on_device(): lax.psum(jnp.sum(term_three * term_three, axis=1), ('grp', 'leaf'))  46.5 us
    all_gather x1, blocking collectives, on_device(): subtree_skel = lax.all_gather(skel_points, 'leaf', axis=0, tiled=True)  21.1 us
    all_gather x1, blocking collectives, on_device(): subtree_lists = lax.all_gather(inter_lists, 'leaf', axis=0, tiled=True)  15.5 us
    another operation x3, loops' own time, operate(): lax.fori_loop(0, live_slots, near_slot, jnp.zeros((per_dev, vec_count, le...  13.7 us
    all_gather x3, blocking collectives, operate(): lax.all_gather(subtree_total[None], 'grp', axis=0, tiled=True)  13.1 us
    dot_general x3, matrix products, operate(): jnp.einsum('jvr,tjrq->tvq', coeffs, push_kernel, precision=highest)  10.4 us
  transfers between devices with their start and end apart: 9, of which 2 were waited for; matrix products, arithmetic and copies ran while one was open for 29% of the time, Pallas kernels for 0%

commit v1 on v0

--- a/solution.py
+++ b/solution.py
@@ -92,7 +92,8 @@
     term_one = (operate(vectors) - centre * vectors) / half_width
     term_two = 2.0 * (operate(term_one) - centre * term_one) / half_width - vectors
     term_three = 2.0 * (operate(term_two) - centre * term_two) / half_width - term_one
-    squares = lax.psum(jnp.sum(term_three * term_three, axis=1), ("grp", "leaf"))
+    half = lax.psum(jnp.sum(term_three * term_three, axis=1), "leaf")
+    squares = lax.psum(half, "grp")
     total_points = vectors.shape[1] * group_count * lax.axis_size("leaf")
     return term_three / jnp.sqrt(squares / total_points + 1e-06)[:, None]
 

time: 313 us -> 312 us (level)
  the two profiles are of different devices: /device:TPU:10 before, /device:TPU:0 now
where the time goes in v1:
time: 312 us; the launch traced here: 311 us
  blocking collectives  190 us (61%)
  matrix products  49.9 us (16%)
  starting transfers between devices  25.4 us (8%)
  local copies, waits for them, and re-layouts  17.3 us (6%)
  between operations  13.7 us (4%)
  loops' own time  10.5 us (3%)
  other arithmetic  3.99 us (1%)
    psum x3, blocking collectives, operate(): subtree_total = lax.psum(upward, 'leaf')  95.2 us
    psum x1, blocking collectives, on_device(): half = lax.psum(jnp.sum(term_three * term_three, axis=1), 'leaf')  36.2 us
    dot_general x12, matrix products, near_slot(): product = jnp.einsum('vlp,lpq->lvq', source_vecs, kernel, precision=highest)  33.3 us
    all_gather x1, blocking collectives, on_device(): subtree_lists = lax.all_gather(inter_lists, 'leaf', axis=0, tiled=True)  23.1 us
    ppermute x3, starting transfers between devices, with_halo(): before = lax.ppermute(last, axis, up)  21.3 us
    all_gather x1, blocking collectives, on_device(): subtree_skel = lax.all_gather(skel_points, 'leaf', axis=0, tiled=True)  17.6 us
    all_gather x3, blocking collectives, operate(): lax.all_gather(subtree_total[None], 'grp', axis=0, tiled=True)  13.1 us
    another operation x3, loops' own time, operate(): lax.fori_loop(0, live_slots, near_slot, jnp.zeros((per_dev, vec_count, le...  10.5 us
  transfers between devices with their start and end apart: 9, of which 0 were waited for; matrix products, arithmetic and copies ran while one was open for 21% of the time, Pallas kernels for 0%

profile of v1, /device:TPU:0, one launch (start us, length us, event | category | flops | bytes accessed | tf_op | source)
XLA Modules:
  0.0 311.1 jit_solution(420931714834345022)
XLA Ops:
  7.5 1.4 collective-permute-start.1
  8.9 3.0 collective-permute-start
  14.4 23.1 %all-gather = s32[16,2,16]{2,1,0:T(2,128)S(1)} all-gather(s32[1,2,16]{2,1,0:T(2,128)S(1)} %bitcast.260), channel_id=1, replica_groups=mesh['grp'=2,'leaf'=16] {'leaf'}, dimensions={0}, use_global_device_ids=true | all-gather | bytes 2176 | tf_op jit(solution)/shard_map/all_gather | solution.py:49
  37.7 17.6 %all_gather.15 = f32[32,3,64]{2,1,0:T(4,128)S(1)} all-gather(f32[2,3,64]{2,1,0:T(4,128)S(1)} %bitcast_select_fusion.1), channel_id=1, replica_groups=mesh['grp'=2,'leaf'=16] {'leaf'}, dimensions={0}, use_global_device_ids=true | all-gather | bytes 26112 | tf_op jit(solution)/shard_map/all_gather | solution.py:43
  55.7 3.5 %convolution_bitcast_fusion.2 = f32[32,16,64]{2,1,0:T(8,128)} fusion(f32[32,2]{1,0:T(8,128)S(1)} %copy.67, f32[32,64]{1,0:T(8,128)S(1)} %bitcast.254, f32[2,64]{1,0:T(2,128)S(1)} %bitcast.264, f32[32,64]{1,0:T(8,128)S(1)} %bitcast.257, f32[2,64]{1,0:T(2,128)S(1)} %bitcast.267, f32[32,64]{1,0:T(8,128)S(1)} %bitcast.251, f32[2,64]{1,0:T(2,128)S(1)} %bitcast.261, ...), kind=kOutput, calls=%fused_computation.145 | convolution fusion | flops 53739520 | bytes 165632 | tf_op jit(solution)/shard_map/jvr,tjrq->tvq/dot_general | solution.py:78
  60.2 31.6 %psum.35 = f32[1,16,128]{2,1,0:T(8,128)S(1)} all-reduce(f32[1,16,128]{2,1,0:T(8,128)S(1)} %convolution_bitcast_fusion.8), channel_id=1, replica_groups=mesh['grp'=2,'leaf'=16] {'leaf'}, use_global_device_ids=true, to_apply=%region_6.9 | all-reduce | flops 2048 | bytes 16384 | tf_op jit(solution)/shard_map/psum | solution.py:84
  91.9 4.4 %all_gather.17 = f32[2,16,128]{2,1,0:T(8,128)S(1)} all-gather(f32[1,16,128]{2,1,0:T(8,128)S(1)} %psum.35), channel_id=1, replica_groups=mesh['grp'=2,'leaf'=16] {'grp'}, dimensions={0}, use_global_device_ids=true | all-gather | bytes 24576 | tf_op jit(solution)/shard_map/all_gather | solution.py:85
  97.6 19.5 %while.30 = (s32[]{:T(128)}, f32[2,16,512]{2,1,0:T(8,128)S(1)}, s32[]{:T(128)}, s32[2,6]{0,1:T(8,128)S(1)}, f32[16,6,512]{2,0,1:T(8,128)S(1)}, /*index=5*/f32[3,...) while((s32[]{:T(128)}, f32[2,16,512]{2,1,0:T(8,128)S(1)}, s32[]{:T(128)}, ...), condition=%wide.region_3.0_spmd, body=%wide.region_2.0_spmd.sunk | while | flops 107008024 | bytes 479441 | solution.py:72
  99.5 2.8 fusion.199
  104.2 2.8 fusion.199
  108.9 2.8 fusion.199
  113.7 2.8 fusion.199
  119.7 9.0 %collective-permute-start.2 = (f32[19,1024]{1,0:T(8,128)S(1)}, f32[19,1024]{1,0:T(8,128)S(1)}, u32[]{:S(2)}, u32[]{:S(2)}) collective-permute-start(f32[19,1024]{1,0:T(8,128)S(1)} %pad_maximum_fusion.4), channel_id=1, source_target_pairs={{0,1},{1,2},{2,3},{3,4},{4,5},{5,6},{6,7},{7,8},{8,9},{9,10},{10,1... | collective-permute-start | bytes 233480 | tf_op jit(solution)/shard_map/ppermute | solution.py:19
  129.1 3.5 %convolution_bitcast_fusion.1 = f32[32,16,64]{2,1,0:T(8,128)} fusion(f32[32,2]{1,0:T(8,128)S(1)} %copy.67, f32[32,64]{1,0:T(8,128)S(1)} %bitcast.255, f32[2,64]{1,0:T(2,128)S(1)} %bitcast.265, f32[32,64]{1,0:T(8,128)S(1)} %bitcast.258, f32[2,64]{1,0:T(2,128)S(1)} %bitcast.268, f32[32,64]{1,0:T(8,128)S(1)} %bitcast.252, f32[2,64]{1,0:T(2,128)S(1)} %bitcast.262, ...), kind=kOutput, calls=%fused_computation.144 | convolution fusion | flops 53739520 | bytes 165632 | tf_op jit(solution)/shard_map/jvr,tjrq->tvq/dot_general | solution.py:78
  132.9 31.8 %psum.36 = f32[1,16,128]{2,1,0:T(8,128)S(1)} all-reduce(f32[1,16,128]{2,1,0:T(8,128)S(1)} %convolution_bitcast_fusion.7), channel_id=1, replica_groups=mesh['grp'=2,'leaf'=16] {'leaf'}, use_global_device_ids=true, to_apply=%region_10.13 | all-reduce | flops 2048 | bytes 16384 | tf_op jit(solution)/shard_map/psum | solution.py:84
  164.7 4.4 %all_gather.18 = f32[2,16,128]{2,1,0:T(8,128)S(1)} all-gather(f32[1,16,128]{2,1,0:T(8,128)S(1)} %psum.36), channel_id=1, replica_groups=mesh['grp'=2,'leaf'=16] {'grp'}, dimensions={0}, use_global_device_ids=true | all-gather | bytes 24576 | tf_op jit(solution)/shard_map/all_gather | solution.py:85
  169.5 19.7 %while.31 = (s32[]{:T(128)}, f32[2,16,512]{2,1,0:T(8,128)S(1)}, s32[]{:T(128)}, s32[2,6]{0,1:T(8,128)S(1)}, f32[16,6,512]{2,0,1:T(8,128)S(1)}, /*index=5*/f32[3,...) while((s32[]{:T(128)}, f32[2,16,512]{2,1,0:T(8,128)S(1)}, s32[]{:T(128)}, ...), condition=%wide.region_8.11_spmd, body=%wide.region_7.10_spmd.sunk | while | flops 107008024 | bytes 479441 | solution.py:72
  171.6 2.8 fusion.203
  176.4 2.8 fusion.203
  181.1 2.8 fusion.203
  185.8 2.8 fusion.203
  191.9 9.2 %collective-permute-start.4 = (f32[19,1024]{1,0:T(8,128)S(1)}, f32[19,1024]{1,0:T(8,128)S(1)}, u32[]{:S(2)}, u32[]{:S(2)}) collective-permute-start(f32[19,1024]{1,0:T(8,128)S(1)} %pad_maximum_fusion.5), channel_id=1, source_target_pairs={{0,1},{1,2},{2,3},{3,4},{4,5},{5,6},{6,7},{7,8},{8,9},{9,10},{10,1... | collective-permute-start | bytes 233480 | tf_op jit(solution)/shard_map/ppermute | solution.py:19
  201.4 3.5 %convolution_bitcast_fusion = f32[32,16,64]{2,1,0:T(8,128)} fusion(f32[32,2]{1,0:T(8,128)S(1)} %copy.67, f32[32,64]{1,0:T(8,128)S(1)} %bitcast.256, f32[2,64]{1,0:T(2,128)S(1)} %bitcast.266, f32[32,64]{1,0:T(8,128)S(1)} %bitcast.259, f32[2,64]{1,0:T(2,128)S(1)} %bitcast.269, f32[32,64]{1,0:T(8,128)S(1)} %bitcast.253, f32[2,64]{1,0:T(2,128)S(1)} %bitcast.263, ...), kind=kOutput, calls=%fused_computation.143 | convolution fusion | flops 53739520 | bytes 165632 | tf_op jit(solution)/shard_map/jvr,tjrq->tvq/dot_general | solution.py:78
  205.1 31.8 %psum.37 = f32[1,16,128]{2,1,0:T(8,128)S(1)} all-reduce(f32[1,16,128]{2,1,0:T(8,128)S(1)} %convolution_bitcast_fusion.6), channel_id=1, replica_groups=mesh['grp'=2,'leaf'=16] {'leaf'}, use_global_device_ids=true, to_apply=%region_14.17 | all-reduce | flops 2048 | bytes 16384 | tf_op jit(solution)/shard_map/psum | solution.py:84
  237.0 4.4 %all_gather.19 = f32[2,16,128]{2,1,0:T(8,128)S(1)} all-gather(f32[1,16,128]{2,1,0:T(8,128)S(1)} %psum.37), channel_id=1, replica_groups=mesh['grp'=2,'leaf'=16] {'grp'}, dimensions={0}, use_global_device_ids=true | all-gather | bytes 24576 | tf_op jit(solution)/shard_map/all_gather | solution.py:85
  241.8 19.5 %while.32 = (s32[]{:T(128)}, f32[2,16,512]{2,1,0:T(8,128)S(1)}, s32[]{:T(128)}, s32[2,6]{0,1:T(8,128)S(1)}, f32[16,6,512]{2,0,1:T(8,128)S(1)}, /*index=5*/f32[3,...) while((s32[]{:T(128)}, f32[2,16,512]{2,1,0:T(8,128)S(1)}, s32[]{:T(128)}, ...), condition=%wide.region_12.15_spmd, body=%wide.region_11.14_spmd.sunk | while | flops 107008024 | bytes 479441 | solution.py:72
  243.7 2.8 fusion.207
  248.5 2.8 fusion.207
  253.2 2.8 fusion.207
  257.9 2.8 fusion.207
  262.8 36.2 %psum.38 = f32[16]{0:T(128)S(1)} all-reduce(f32[16]{0:T(128)S(1)} %multiply_reduce_fusion), channel_id=1, replica_groups=mesh['grp'=2,'leaf'=16] {'leaf'}, use_global_device_ids=true, to_apply=%region_16.19 | all-reduce | flops 16 | bytes 128 | tf_op jit(solution)/shard_map/psum | solution.py:95
  299.0 4.9 %psum.39 = f32[16]{0:T(128)S(1)} all-reduce(f32[16]{0:T(128)S(1)} %psum.38), channel_id=1, replica_groups=mesh['grp'=2,'leaf'=16] {'grp'}, use_global_device_ids=true, to_apply=%region_17.20 | all-reduce | flops 16 | bytes 128 | tf_op jit(solution)/shard_map/psum | solution.py:96
  (191 shorter events, 30.3 us)
Async XLA Ops:
  6.5 48.8 %copy-start = (f32[2,64,512]{2,1,0:T(8,128)S(1)}, f32[2,64,512]{2,1,0:T(8,128)}, u32[]{:S(2)}) copy-start(f32[2,64,512]{2,1,0:T(8,128)} %param.23) | copy-start | bytes 786436
  6.5 6.4 %copy-start.7 = (s32[2,64]{1,0:T(2,128)S(1)}, s32[2,64]{1,0:T(2,128)}, u32[]{:S(2)}) copy-start(s32[2,64]{1,0:T(2,128)} %param.22) | copy-start | bytes 1540
  6.5 7.8 %copy-start.5 = (s32[2,16]{1,0:T(2,128)S(1)}, s32[2,16]{1,0:T(2,128)}, u32[]{:S(2)}) copy-start(s32[2,16]{1,0:T(2,128)} %param.21) | copy-start | bytes 388
  6.5 110.6 %reduce-scatter.4.cloned.1.call-start = ((), (), s32[]{:S(2)}) async-start(), calls=%async_computation.3 | async-start | bytes 278528 | tf_op jit(solution)/shard_map/reduce_scatter | solution.py:77
  7.5 47.9 %copy-start.2 = (f32[16,1024]{1,0:T(8,128)S(1)}, f32[16,1024]{1,0:T(8,128)}, u32[]{:S(2)}) copy-start(f32[16,1024]{1,0:T(8,128)} %param.18) | copy-start | bytes 196612
  7.5 90.0 %collective-permute-start.1 = (f32[19,1024]{1,0:T(8,128)S(1)}, f32[19,1024]{1,0:T(8,128)S(1)}, u32[]{:S(2)}, u32[]{:S(2)}) collective-permute-start(f32[19,1024]{1,0:T(8,128)S(1)} %pad_maximum_fusion.3), channel_id=1, source_target_pairs={{1,0},{2,1},{3,2},{4,3},{5,4},{6,5},{7,6},{8,7},{9,8},{10,9},{11,1... | collective-permute-start | bytes 233480 | tf_op jit(solution)/shard_map/ppermute | solution.py:20
  8.9 88.5 %collective-permute-start = (f32[19,1024]{1,0:T(8,128)S(1)}, f32[19,1024]{1,0:T(8,128)S(1)}, u32[]{:S(2)}, u32[]{:S(2)}) collective-permute-start(f32[19,1024]{1,0:T(8,128)S(1)} %pad_maximum_fusion.3), channel_id=1, source_target_pairs={{0,1},{1,2},{2,3},{3,4},{4,5},{5,6},{6,7},{7,8},{8,9},{9,10},{10,1... | collective-permute-start | bytes 233480 | tf_op jit(solution)/shard_map/ppermute | solution.py:19
  59.2 0.7 copy-start.6
  59.2 0.9 copy-start.1
  59.2 37.1 %copy-start.4 = (f32[2,3,128]{2,0,1:T(2,128)S(1)}, f32[2,3,128]{2,0,1:T(2,128)}, u32[]{:S(2)}) copy-start(f32[2,3,128]{2,0,1:T(2,128)} %param.25) | copy-start | bytes 9220
  59.2 38.2 %copy-start.3 = (f32[3,1024]{1,0:T(4,128)S(1)}, f32[3,1024]{1,0:T(4,128)}, u32[]{:S(2)}) copy-start(f32[3,1024]{1,0:T(4,128)} %param.19) | copy-start | bytes 36868
  59.2 130.0 %reduce-scatter.6.cloned.1.call-start = ((), (), s32[]{:S(2)}) async-start(), calls=%async_computation.4 | async-start | bytes 278528 | tf_op jit(solution)/shard_map/reduce_scatter | solution.py:77
  118.4 51.0 %collective-permute-start.3 = (f32[19,1024]{1,0:T(8,128)S(1)}, f32[19,1024]{1,0:T(8,128)S(1)}, u32[]{:S(2)}, u32[]{:S(2)}) collective-permute-start(f32[19,1024]{1,0:T(8,128)S(1)} %pad_maximum_fusion.4), channel_id=1, source_target_pairs={{1,0},{2,1},{3,2},{4,3},{5,4},{6,5},{7,6},{8,7},{9,8},{10,9},{11,1... | collective-permute-start | bytes 233480 | tf_op jit(solution)/shard_map/ppermute | solution.py:20
  119.7 49.7 %collective-permute-start.2 = (f32[19,1024]{1,0:T(8,128)S(1)}, f32[19,1024]{1,0:T(8,128)S(1)}, u32[]{:S(2)}, u32[]{:S(2)}) collective-permute-start(f32[19,1024]{1,0:T(8,128)S(1)} %pad_maximum_fusion.4), channel_id=1, source_target_pairs={{0,1},{1,2},{2,3},{3,4},{4,5},{5,6},{6,7},{7,8},{8,9},{9,10},{10,1... | collective-permute-start | bytes 233480 | tf_op jit(solution)/shard_map/ppermute | solution.py:19
  132.8 128.6 %reduce-scatter.8.cloned.1.call-start = ((), (), s32[]{:S(2)}) async-start(), calls=%async_computation.5 | async-start | bytes 278528 | tf_op jit(solution)/shard_map/reduce_scatter | solution.py:77
  190.6 51.1 %collective-permute-start.5 = (f32[19,1024]{1,0:T(8,128)S(1)}, f32[19,1024]{1,0:T(8,128)S(1)}, u32[]{:S(2)}, u32[]{:S(2)}) collective-permute-start(f32[19,1024]{1,0:T(8,128)S(1)} %pad_maximum_fusion.5), channel_id=1, source_target_pairs={{1,0},{2,1},{3,2},{4,3},{5,4},{6,5},{7,6},{8,7},{9,8},{10,9},{11,1... | collective-permute-start | bytes 233480 | tf_op jit(solution)/shard_map/ppermute | solution.py:20
  191.9 49.8 %collective-permute-start.4 = (f32[19,1024]{1,0:T(8,128)S(1)}, f32[19,1024]{1,0:T(8,128)S(1)}, u32[]{:S(2)}, u32[]{:S(2)}) collective-permute-start(f32[19,1024]{1,0:T(8,128)S(1)} %pad_maximum_fusion.5), channel_id=1, source_target_pairs={{0,1},{1,2},{2,3},{3,4},{4,5},{5,6},{6,7},{7,8},{8,9},{9,10},{10,1... | collective-permute-start | bytes 233480 | tf_op jit(solution)/shard_map/ppermute | solution.py:19
Sparse Core Ops, SparseCore 0:
  59.3 54.1 reduce-scatter.3
  132.9 54.3 reduce-scatter.5
  205.3 54.3 reduce-scatter.7
